TPU v7x, 32 devices: a whole 2x2x4 slice. The times are simulated.
32 devices in a mesh: dp: 8 (over y, x, core), tensor: 4 (over z).
Axes of the slice: x: 2, y: 2, z: 4, core: 2. Of those that a mesh axis runs over, the one named last changes fastest.
Arguments:
- tokens: bfloat16 [16, 1024, 1024], P('dp', 'tensor'), may hold values from -6 to 6
- segments: int32 [16, 1024], P('dp'), may hold values from 0 to 3, as said below
- qkv_weight: bfloat16 [3, 1024, 1024], P(None, None, 'tensor'), may hold values from -0.1875 to 0.1875
- qkv_bias: float32 [3, 1024], P(None, 'tensor'), may hold values from -1.5 to 1.5
- out_weight: bfloat16 [1024, 1024], P('tensor'), may hold values from -0.75 to 0.75
- out_bias: float32 [1024], replicated, may hold values from -1.5 to 1.5
- gain_one: float32 [1024], replicated, may hold values from 0.5 to 1.5
- shift_one: float32 [1024], replicated, may hold values from -1.5 to 1.5
- up_weight: bfloat16 [1024, 4096], P(None, 'tensor'), may hold values from -0.1875 to 0.1875
- up_bias: float32 [4096], P('tensor'), may hold values from -1.5 to 1.5
- down_weight: bfloat16 [4096, 1024], P('tensor'), may hold values from -0.1875 to 0.1875
- down_bias: float32 [1024], replicated, may hold values from -1.5 to 1.5
- gain_two: float32 [1024], replicated, may hold values from 0.5 to 1.5
- shift_two: float32 [1024], replicated, may hold values from -1.5 to 1.5
- proj_weight: bfloat16 [1024, 288], replicated, may hold values from -0.1875 to 0.1875
- out_grad: bfloat16 [16, 1024, 1024], P('dp', 'tensor'), may hold values from -6 to 6
- embed_grad: bfloat16 [16, 1024, 288], P('dp', 'tensor'), may hold values from -6 to 6
Outputs:
- layer_out: bfloat16 [16, 1024, 1024], P('dp', 'tensor')
- embeddings: bfloat16 [16, 1024, 288], P('dp', 'tensor')
- tokens_grad: float32 [16, 1024, 1024], P('dp', 'tensor')
- qkv_weight_grad: float32 [3, 1024, 1024], P(None, None, 'tensor')
- qkv_bias_grad: float32 [3, 1024], P(None, 'tensor')
- out_weight_grad: float32 [1024, 1024], P('tensor')
- out_bias_grad: float32 [1024], replicated
- gain_one_grad: float32 [1024], replicated
- shift_one_grad: float32 [1024], replicated
- up_weight_grad: float32 [1024, 4096], P(None, 'tensor')
- up_bias_grad: float32 [4096], P('tensor')
- down_weight_grad: float32 [4096, 1024], P('tensor')
- down_bias_grad: float32 [1024], replicated
- gain_two_grad: float32 [1024], replicated
- shift_two_grad: float32 [1024], replicated
- proj_weight_grad: float32 [1024, 288], replicated
Inputs may be any that keep to these rules, and one draw needn't show every extreme that they name: `segments`: segment numbers never fall along a sequence; every sequence holds 4 documents, each of at least 200 tokens, and in every sequence some document has exactly 200.
All inputs are finite; a program needn't handle non-finite values.
Results may differ from a plain program's by a relative error of at most 0.018.
Values may be sent and summed in bfloat16 or wider, within the bound.
A program may use at most 192 MiB of HBM per device.

v0:
```python
import math
import jax
import jax.numpy as jnp
from jax import lax
from jax.sharding import PartitionSpec as P

HEAD_DIM = 64
eps = 1e-05


def as_sent(array):

    def short(part):
        return part.astype(jnp.bfloat16) if part.dtype == jnp.float32 else part

    return jax.tree.map(short, array)


def doc_positions(segment_rows):
    length = segment_rows.shape[-1]
    row_index = jnp.broadcast_to(jnp.arange(length, dtype=jnp.int32), segment_rows.shape)
    change = jnp.concatenate(
        [
            jnp.ones(segment_rows.shape[:-1] + (1,), jnp.bool_),
            segment_rows[..., 1:] != segment_rows[..., :-1],
        ],
        axis=-1,
    )
    doc_start = lax.cummax(
        jnp.where(change, row_index, jnp.zeros_like(row_index)), axis=segment_rows.ndim - 1
    )
    return row_index - doc_start


def rotary_tables(positions, head_dim):
    half_dim = head_dim // 2
    exponent = jnp.arange(half_dim, dtype=jnp.float32) * (2.0 / head_dim)
    frequency = jnp.exp(-exponent * math.log(10000.0))
    angles = positions.astype(jnp.float32)[..., None] * frequency
    angles = jnp.concatenate([angles, angles], axis=-1)
    return (jnp.cos(angles), jnp.sin(angles))


def rotate(field, cosine, sine):
    half_dim = field.shape[-1] // 2
    rotated = jnp.concatenate([-field[..., half_dim:], field[..., :half_dim]], axis=-1)
    return field * cosine + rotated * sine


def rotate_back(field, cosine, sine):
    half_dim = field.shape[-1] // 2
    rotated = jnp.concatenate([-field[..., half_dim:], field[..., :half_dim]], axis=-1)
    return field * cosine - rotated * sine


def norm_forward(field, gain, shift):
    row_mean = jnp.mean(field, axis=-1, keepdims=True)
    centred = field - row_mean
    variance = jnp.mean(centred * centred, axis=-1, keepdims=True)
    inv_std = lax.rsqrt(variance + eps)
    scaled = centred * inv_std
    return (scaled * gain + shift, scaled, inv_std)


def norm_backward(upstream, scaled, inv_std, gain):
    grad_scaled = upstream * gain
    grad_input = inv_std * (
        grad_scaled
        - jnp.mean(grad_scaled, axis=-1, keepdims=True)
        - scaled * jnp.mean(grad_scaled * scaled, axis=-1, keepdims=True)
    )
    return (grad_input, jnp.sum(upstream * scaled, axis=(0, 1)), jnp.sum(upstream, axis=(0, 1)))


def device_rows(full_rows, row_count):
    groups, length, model_width = full_rows.shape
    local_rows = length // lax.axis_size("tensor")
    blocks = row_count // (groups * local_rows)
    picked = full_rows
    picked = picked.reshape(groups, blocks, local_rows, model_width).transpose(1, 0, 2, 3)
    return picked.reshape(row_count, model_width)


def masked_scores(queries, keys, seg_row):
    scores = jnp.einsum("hqd,hkd->hqk", queries, keys, preferred_element_type=jnp.float32)
    same_doc = seg_row[:, None] == seg_row[None, :]
    return jnp.where(same_doc[None], scores, -1000000000.0)


def attend(inputs):
    queries, keys, values_low, seg_row = inputs
    scores = masked_scores(queries, keys, seg_row)
    row_peak = jnp.max(scores, axis=-1, keepdims=True)
    shifted = jnp.exp(scores - row_peak)
    row_total = jnp.sum(shifted, axis=-1, keepdims=True)
    probs = (shifted / row_total).astype(jnp.bfloat16)
    mixed_heads = jnp.einsum("hqk,hkd->hqd", probs, values_low, preferred_element_type=jnp.float32)
    return (mixed_heads, row_peak + jnp.log(row_total))


def attend_back(inputs):
    queries, keys, values_low, seg_row, log_total, grad_mixed = inputs
    scores = masked_scores(queries, keys, seg_row)
    probs = jnp.exp(scores - log_total)
    grad_values = jnp.einsum(
        "hqk,hqd->hkd", probs.astype(jnp.bfloat16), grad_mixed, preferred_element_type=jnp.float32
    )
    grad_probs = jnp.einsum(
        "hqd,hkd->hqk", grad_mixed, values_low, preferred_element_type=jnp.float32
    )
    row_inner = jnp.sum(probs * grad_probs, axis=-1, keepdims=True)
    grad_scores = (probs * (grad_probs - row_inner)).astype(jnp.bfloat16)
    grad_queries = jnp.einsum("hqk,hkd->hqd", grad_scores, keys, preferred_element_type=jnp.float32)
    grad_keys = jnp.einsum("hqk,hqd->hkd", grad_scores, queries, preferred_element_type=jnp.float32)
    return (grad_queries, grad_keys, grad_values)


def process(tokens, segments, out_grad, embed_grad, weights):
    (
        qkv_weight,
        qkv_bias,
        out_weight,
        out_bias,
        gain_one,
        shift_one,
        up_weight,
        up_bias,
        down_weight,
        down_bias,
        gain_two,
        shift_two,
        proj_weight,
    ) = weights
    groups, local_rows, model_width = tokens.shape
    length = segments.shape[1]
    heads_here = qkv_weight.shape[2] // HEAD_DIM
    q_scale = HEAD_DIM ** (-0.5)
    cosine, sine = rotary_tables(doc_positions(segments), HEAD_DIM)
    cosine = cosine[:, None]
    sine = sine[:, None]

    def split_heads(field):
        return field.reshape(groups, length, heads_here, HEAD_DIM).transpose(0, 2, 1, 3)

    def join_heads(field):
        return field.transpose(0, 2, 1, 3).reshape(groups, length, heads_here * HEAD_DIM)

    whole_tokens = lax.all_gather(tokens, "tensor", axis=1, tiled=True)
    projected = jnp.einsum(
        "gld,cde->cgle", whole_tokens, qkv_weight, preferred_element_type=jnp.float32
    )
    projected = projected + qkv_bias[:, None, None, :]
    queries = (rotate(split_heads(projected[0]), cosine, sine) * q_scale).astype(jnp.bfloat16)
    keys = rotate(split_heads(projected[1]), cosine, sine).astype(jnp.bfloat16)
    values_low = split_heads(projected[2]).astype(jnp.bfloat16)
    mixed_heads, log_total = lax.map(attend, (queries, keys, values_low, segments))
    mixed = join_heads(mixed_heads).astype(jnp.bfloat16)
    attn_part = lax.psum_scatter(
        jnp.dot(
            device_rows(mixed, lax.axis_size("tensor") * (groups * local_rows)),
            out_weight,
            preferred_element_type=jnp.float32,
        ),
        "tensor",
        scatter_dimension=0,
        tiled=True,
    )
    attn_part = attn_part.reshape(groups, local_rows, model_width)
    first_sum = tokens.astype(jnp.float32) + (attn_part + out_bias)
    normed, scaled_one, inv_one = norm_forward(first_sum, gain_one, shift_one)
    whole_normed = lax.all_gather(normed.astype(jnp.bfloat16), "tensor", axis=1, tiled=True)
    hidden = (
        jnp.einsum("gld,df->glf", whole_normed, up_weight, preferred_element_type=jnp.float32)
        + up_bias
    )
    active = jax.nn.gelu(hidden, approximate=False).astype(jnp.bfloat16)
    ffn_part = lax.psum_scatter(
        jnp.dot(
            device_rows(active, lax.axis_size("tensor") * (groups * local_rows)),
            down_weight,
            preferred_element_type=jnp.float32,
        ),
        "tensor",
        scatter_dimension=0,
        tiled=True,
    )
    second_sum = normed + (ffn_part.reshape(groups, local_rows, model_width) + down_bias)
    result, scaled_two, inv_two = norm_forward(second_sum, gain_two, shift_two)
    result_low = result.astype(jnp.bfloat16)
    embedded = jnp.einsum(
        "gld,dp->glp", result_low, proj_weight, preferred_element_type=jnp.float32
    )
    grad_result = out_grad.astype(jnp.float32) + jnp.einsum(
        "glp,dp->gld", embed_grad, proj_weight, preferred_element_type=jnp.float32
    )
    proj_grad = jnp.einsum(
        "gld,glp->dp", result_low, embed_grad, preferred_element_type=jnp.float32
    )
    grad_second, gain_two_grad, shift_two_grad = norm_backward(
        grad_result, scaled_two, inv_two, gain_two
    )
    second_low = grad_second.astype(jnp.bfloat16)
    down_bias_grad = jnp.sum(second_low.astype(jnp.float32), axis=(0, 1))
    whole_second = lax.all_gather(second_low, "tensor", axis=1, tiled=True)
    down_weight_grad = jnp.einsum(
        "glf,gld->fd", active, whole_second, preferred_element_type=jnp.float32
    )
    grad_active = jnp.einsum(
        "gld,fd->glf", whole_second, down_weight, preferred_element_type=jnp.float32
    )
    gelu_pull = jax.vjp(lambda field: jax.nn.gelu(field, approximate=False), hidden)[1]
    grad_hidden = gelu_pull(grad_active)[0].astype(jnp.bfloat16)
    up_bias_grad = jnp.sum(grad_hidden.astype(jnp.float32), axis=(0, 1))
    up_weight_grad = jnp.einsum(
        "gld,glf->df", whole_normed, grad_hidden, preferred_element_type=jnp.float32
    )
    ffn_back = lax.psum_scatter(
        jnp.einsum(
            "nf,df->nd",
            device_rows(grad_hidden, lax.axis_size("tensor") * (groups * local_rows)),
            up_weight,
            preferred_element_type=jnp.float32,
        ),
        "tensor",
        scatter_dimension=0,
        tiled=True,
    )
    grad_normed = grad_second + ffn_back.reshape(groups, local_rows, model_width)
    grad_first, gain_one_grad, shift_one_grad = norm_backward(
        grad_normed, scaled_one, inv_one, gain_one
    )
    first_low = grad_first.astype(jnp.bfloat16)
    out_bias_grad = jnp.sum(first_low.astype(jnp.float32), axis=(0, 1))
    whole_first = lax.all_gather(first_low, "tensor", axis=1, tiled=True)
    out_weight_grad = jnp.einsum(
        "glh,gld->hd", mixed, whole_first, preferred_element_type=jnp.float32
    )
    grad_mixed = jnp.einsum(
        "gld,hd->glh", whole_first, out_weight, preferred_element_type=jnp.float32
    )
    grad_mixed = split_heads(grad_mixed.astype(jnp.bfloat16))
    grad_queries, grad_keys, grad_values = lax.map(
        attend_back, (queries, keys, values_low, segments, log_total, grad_mixed)
    )
    grad_queries = rotate_back(grad_queries * q_scale, cosine, sine)
    grad_keys = rotate_back(grad_keys, cosine, sine)
    grad_qkv = jnp.stack(
        [join_heads(grad_queries), join_heads(grad_keys), join_heads(grad_values)]
    ).astype(jnp.bfloat16)
    qkv_bias_grad = jnp.sum(grad_qkv.astype(jnp.float32), axis=(1, 2))
    qkv_weight_grad = jnp.einsum(
        "gld,cgle->cde", whole_tokens, grad_qkv, preferred_element_type=jnp.float32
    )
    joined_grad = grad_qkv.transpose(1, 2, 0, 3).reshape(groups, length, 3 * heads_here * HEAD_DIM)
    joined_weight = qkv_weight.transpose(1, 0, 2).reshape(model_width, 3 * heads_here * HEAD_DIM)
    input_back = lax.psum_scatter(
        jnp.einsum(
            "ne,de->nd",
            device_rows(joined_grad, groups * local_rows * lax.axis_size("tensor")),
            joined_weight,
            preferred_element_type=jnp.float32,
        ).astype(jnp.bfloat16),
        "tensor",
        scatter_dimension=0,
        tiled=True,
    ).astype(jnp.float32)
    tokens_grad = grad_first + input_back.reshape(groups, local_rows, model_width)
    sharded_grads = (
        qkv_weight_grad,
        qkv_bias_grad,
        out_weight_grad,
        up_weight_grad,
        up_bias_grad,
        down_weight_grad,
    )
    shared_grads = (
        out_bias_grad,
        gain_one_grad,
        shift_one_grad,
        down_bias_grad,
        gain_two_grad,
        shift_two_grad,
        proj_grad,
    )
    return (result_low, embedded.astype(jnp.bfloat16), tokens_grad, sharded_grads, shared_grads)


def per_device(
    tokens,
    segments,
    qkv_weight,
    qkv_bias,
    out_weight,
    out_bias,
    gain_one,
    shift_one,
    up_weight,
    up_bias,
    down_weight,
    down_bias,
    gain_two,
    shift_two,
    proj_weight,
    out_grad,
    embed_grad,
):
    weights = (
        qkv_weight,
        qkv_bias,
        out_weight,
        out_bias,
        gain_one,
        shift_one,
        up_weight,
        up_bias,
        down_weight,
        down_bias,
        gain_two,
        shift_two,
        proj_weight,
    )

    def one_seq(running, per_seq):
        tok_row, seg_row, dy_row, de_row = per_seq
        results = process(tok_row[None], seg_row[None], dy_row[None], de_row[None], weights)
        running = jax.tree.map(jnp.add, running, (results[3], results[4]))
        return (running, (results[0][0], results[1][0], results[2][0]))

    empty_grads = (
        tuple(
            (
                jnp.zeros(w.shape, jnp.float32)
                for w in (qkv_weight, qkv_bias, out_weight, up_weight, up_bias, down_weight)
            )
        ),
        tuple(
            (
                jnp.zeros(w.shape, jnp.float32)
                for w in (
                    out_bias,
                    gain_one,
                    shift_one,
                    down_bias,
                    gain_two,
                    shift_two,
                    proj_weight,
                )
            )
        ),
    )
    (sharded_grads, shared_grads), (layer_out, embeddings, tokens_grad) = lax.scan(
        one_seq, empty_grads, (tokens, segments, out_grad, embed_grad)
    )
    sharded_grads = jax.tree.map(
        lambda part: part.astype(jnp.float32), lax.psum(as_sent(sharded_grads), "dp")
    )
    shared_grads = lax.psum(shared_grads, ("dp", "tensor"))
    return (
        layer_out,
        embeddings,
        tokens_grad,
        sharded_grads[0],
        sharded_grads[1],
        sharded_grads[2],
        shared_grads[0],
        shared_grads[1],
        shared_grads[2],
        sharded_grads[3],
        sharded_grads[4],
        sharded_grads[5],
        shared_grads[3],
        shared_grads[4],
        shared_grads[5],
        shared_grads[6],
    )


def solution(mesh):
    in_specs = (
        P("dp", "tensor", None),
        P("dp", None),
        P(None, None, "tensor"),
        P(None, "tensor"),
        P("tensor", None),
        P(),
        P(),
        P(),
        P(None, "tensor"),
        P("tensor"),
        P("tensor", None),
        P(),
        P(),
        P(),
        P(),
        P("dp", "tensor", None),
        P("dp", "tensor", None),
    )
    out_specs = (
        P("dp", "tensor", None),
        P("dp", "tensor", None),
        P("dp", "tensor", None),
        P(None, None, "tensor"),
        P(None, "tensor"),
        P("tensor", None),
        P(),
        P(),
        P(),
        P(None, "tensor"),
        P("tensor"),
        P("tensor", None),
        P(),
        P(),
        P(),
        P(),
    )
    return jax.shard_map(
        per_device, mesh=mesh, in_specs=in_specs, out_specs=out_specs, check_vma=False
    )
```

profile of v0, /device:TPU:0, one launch (start us, length us, event | category | flops | bytes accessed | tf_op | source)
XLA Modules:
  0.0 1448.8 jit_solution(7580111649799563815)
XLA Ops:
  10.8 1174.9 %while.6 = (s32[]{:T(128)}, f32[3,1024,256]{1,2,0:T(8,128)}, f32[3,256]{1,0:T(4,128)}, f32[256,1024]{1,0:T(8,128)}, f32[1024,1024]{1,0:T(8,128)}, /*index=5*/f32...) while((s32[]{:T(128)}, f32[3,1024,256]{1,2,0:T(8,128)}, ...), condition=%wide.region_26.27_spmd.clone, body=%wide.region_0.26_spmd.clone.sunk | while | flops 23216961536 | bytes 635246848 | solution.py:351
  17.6 44.3 %all-gather.5.cloned.1.call-done = bf16[1,1024,1024]{2,1,0:T(8,128)(2,1)} async-done(((bf16[1,256,1024]{2,1,0:T(8,128)(2,1)}), bf16[1,1024,1024]{2,1,0:T(8,128)(2,1)}) %all-gather.5.cloned.1.call-update) | async-done | bytes 2097168 | tf_op jit(solution)/shard_map/while/body/eval_jaxpr/all_gather | solution.py:148
  74.1 8.8 fusion.227
  95.1 75.3 %reduce-scatter.5.cloned.1.call-done = f32[256,1024]{1,0:T(8,128)} async-done(((f32[1024,1024]{1,0:T(8,128)}), f32[256,1024]{1,0:T(8,128)}) %reduce-scatter.5.cloned.1.call-update) | async-done | bytes 1048592 | tf_op jit(solution)/shard_map/while/body/eval_jaxpr/reduce_scatter | solution.py:158
  173.2 46.6 %all-gather.7.cloned.1.call-done = bf16[1,1024,1024]{2,1,0:T(8,128)(2,1)} async-done(((bf16[1,256,1024]{2,1,0:T(8,128)(2,1)}), bf16[1,1024,1024]{2,1,0:T(8,128)(2,1)}) %all-gather.7.cloned.1.call-update) | async-done | bytes 2097168 | tf_op jit(solution)/shard_map/while/body/eval_jaxpr/all_gather | solution.py:171
  219.8 14.8 %multiply_convert_fusion.4 = (bf16[1024,1024]{1,0:T(8,128)(2,1)S(1)}, f32[1024,1024]{1,0:T(8,128)}, f32[1024,1024]{1,0:T(8,128)}) fusion(f32[1024]{0:T(1024)S(1)} %copy-done.58, bf16[1024,1024]{1,0:T(8,128)(2,1)} %get-tuple-element.999, bf16[1,1024,1024]{2,1,0:T(8,128)(2,1)} %all-gather.7.cloned.1.call-done), kind=kOutput, calls=%fused_computation.17.clone.1 | convolution fusion | flops 2216689664 | bytes 14684160 | tf_op jit(solution)/shard_map/while/body/eval_jaxpr/gld,df->glf/dot_general | solution.py:173
  240.3 75.6 %reduce-scatter.7.cloned.1.call-done = f32[256,1024]{1,0:T(8,128)} async-done(((f32[1024,1024]{1,0:T(8,128)}), f32[256,1024]{1,0:T(8,128)}) %reduce-scatter.7.cloned.1.call-update) | async-done | bytes 1048592 | tf_op jit(solution)/shard_map/while/body/eval_jaxpr/reduce_scatter | solution.py:177
  322.1 46.0 %all-gather.9.cloned.1.call-done = bf16[1,1024,1024]{2,1,0:T(8,128)(2,1)} async-done(((bf16[1,256,1024]{2,1,0:T(8,128)(2,1)}), bf16[1,1024,1024]{2,1,0:T(8,128)(2,1)}) %all-gather.9.cloned.1.call-update) | async-done | bytes 2097168 | tf_op jit(solution)/shard_map/while/body/eval_jaxpr/all_gather | solution.py:204
  368.0 8.5 convert_reduce_fusion.9
  382.3 75.6 %reduce-scatter.9.cloned.1.call-done = f32[256,1024]{1,0:T(8,128)} async-done(((f32[1024,1024]{1,0:T(8,128)}), f32[256,1024]{1,0:T(8,128)}) %reduce-scatter.9.cloned.1.call-update) | async-done | bytes 1048592 | tf_op jit(solution)/shard_map/while/body/eval_jaxpr/reduce_scatter | solution.py:217
  461.7 46.5 %all-gather.11.cloned.1.call-done = bf16[1,1024,1024]{2,1,0:T(8,128)(2,1)} async-done(((bf16[1,256,1024]{2,1,0:T(8,128)(2,1)}), bf16[1,1024,1024]{2,1,0:T(8,128)(2,1)}) %all-gather.11.cloned.1.call-update) | async-done | bytes 2097168 | tf_op jit(solution)/shard_map/while/body/eval_jaxpr/all_gather | solution.py:234
  510.6 8.7 fusion.236
  519.4 11.8 multiply_reduce_fusion.18
  531.2 12.2 multiply_convert_fusion.5
  576.4 19.7 %reduce-scatter.11.cloned.1.call-done = bf16[256,1024]{1,0:T(8,128)(2,1)} async-done(((bf16[1024,1024]{1,0:T(8,128)(2,1)}), bf16[256,1024]{1,0:T(8,128)(2,1)}) %reduce-scatter.11.cloned.1.call-update) | async-done | bytes 524304 | tf_op jit(solution)/shard_map/while/body/eval_jaxpr/reduce_scatter | solution.py:256
  605.3 40.9 %all-gather.5.cloned.1.call-done = bf16[1,1024,1024]{2,1,0:T(8,128)(2,1)} async-done(((bf16[1,256,1024]{2,1,0:T(8,128)(2,1)}), bf16[1,1024,1024]{2,1,0:T(8,128)(2,1)}) %all-gather.5.cloned.1.call-update) | async-done | bytes 2097168 | tf_op jit(solution)/shard_map/while/body/eval_jaxpr/all_gather | solution.py:148
  658.5 8.8 fusion.227
  679.5 75.1 %reduce-scatter.5.cloned.1.call-done = f32[256,1024]{1,0:T(8,128)} async-done(((f32[1024,1024]{1,0:T(8,128)}), f32[256,1024]{1,0:T(8,128)}) %reduce-scatter.5.cloned.1.call-update) | async-done | bytes 1048592 | tf_op jit(solution)/shard_map/while/body/eval_jaxpr/reduce_scatter | solution.py:158
  757.5 46.6 %all-gather.7.cloned.1.call-done = bf16[1,1024,1024]{2,1,0:T(8,128)(2,1)} async-done(((bf16[1,256,1024]{2,1,0:T(8,128)(2,1)}), bf16[1,1024,1024]{2,1,0:T(8,128)(2,1)}) %all-gather.7.cloned.1.call-update) | async-done | bytes 2097168 | tf_op jit(solution)/shard_map/while/body/eval_jaxpr/all_gather | solution.py:171
  804.1 14.8 %multiply_convert_fusion.4 = (bf16[1024,1024]{1,0:T(8,128)(2,1)S(1)}, f32[1024,1024]{1,0:T(8,128)}, f32[1024,1024]{1,0:T(8,128)}) fusion(f32[1024]{0:T(1024)S(1)} %copy-done.58, bf16[1024,1024]{1,0:T(8,128)(2,1)} %get-tuple-element.999, bf16[1,1024,1024]{2,1,0:T(8,128)(2,1)} %all-gather.7.cloned.1.call-done), kind=kOutput, calls=%fused_computation.17.clone.1 | convolution fusion | flops 2216689664 | bytes 14684160 | tf_op jit(solution)/shard_map/while/body/eval_jaxpr/gld,df->glf/dot_general | solution.py:173
  824.6 75.6 %reduce-scatter.7.cloned.1.call-done = f32[256,1024]{1,0:T(8,128)} async-done(((f32[1024,1024]{1,0:T(8,128)}), f32[256,1024]{1,0:T(8,128)}) %reduce-scatter.7.cloned.1.call-update) | async-done | bytes 1048592 | tf_op jit(solution)/shard_map/while/body/eval_jaxpr/reduce_scatter | solution.py:177
  906.0 46.4 %all-gather.9.cloned.1.call-done = bf16[1,1024,1024]{2,1,0:T(8,128)(2,1)} async-done(((bf16[1,256,1024]{2,1,0:T(8,128)(2,1)}), bf16[1,1024,1024]{2,1,0:T(8,128)(2,1)}) %all-gather.9.cloned.1.call-update) | async-done | bytes 2097168 | tf_op jit(solution)/shard_map/while/body/eval_jaxpr/all_gather | solution.py:204
  966.6 75.6 %reduce-scatter.9.cloned.1.call-done = f32[256,1024]{1,0:T(8,128)} async-done(((f32[1024,1024]{1,0:T(8,128)}), f32[256,1024]{1,0:T(8,128)}) %reduce-scatter.9.cloned.1.call-update) | async-done | bytes 1048592 | tf_op jit(solution)/shard_map/while/body/eval_jaxpr/reduce_scatter | solution.py:217
  1046.0 46.5 %all-gather.11.cloned.1.call-done = bf16[1,1024,1024]{2,1,0:T(8,128)(2,1)} async-done(((bf16[1,256,1024]{2,1,0:T(8,128)(2,1)}), bf16[1,1024,1024]{2,1,0:T(8,128)(2,1)}) %all-gather.11.cloned.1.call-update) | async-done | bytes 2097168 | tf_op jit(solution)/shard_map/while/body/eval_jaxpr/all_gather | solution.py:234
  1095.0 8.7 fusion.236
  1103.7 11.8 multiply_reduce_fusion.18
  1115.5 12.3 multiply_convert_fusion.5
  1163.0 17.5 %reduce-scatter.11.cloned.1.call-done = bf16[256,1024]{1,0:T(8,128)(2,1)} async-done(((bf16[1024,1024]{1,0:T(8,128)(2,1)}), bf16[256,1024]{1,0:T(8,128)(2,1)}) %reduce-scatter.11.cloned.1.call-update) | async-done | bytes 524304 | tf_op jit(solution)/shard_map/while/body/eval_jaxpr/reduce_scatter | solution.py:256
  1197.3 13.8 all-reduce.1
  1212.2 40.5 %all-reduce = (f32[1024]{0:T(1024)}, f32[1024]{0:T(1024)}, f32[1024]{0:T(1024)}, f32[1024]{0:T(1024)}, f32[1024]{0:T(1024)}, /*index=5*/f32[1024]{0:T(1024)}) all-reduce(f32[1024]{0:T(1024)S(1)} %copy-done.49, f32[1024]{0:T(1024)S(1)} %copy-done.46, f32[1024]{0:T(1024)S(1)} %copy-done.43, ...), channel_id=1, replica_groups=mesh['dp'=8,'tensor'=4] {'dp','tensor'}, use_global_device_ids=true, to_apply=%region_30.31 | all-reduce | flops 6144 | bytes 49152 | tf_op jit(solution)/shard_map/psum | solution.py:357
  1252.7 48.6 %all-reduce.8.cloned.1.call-done = (bf16[3,1024,256]{2,1,0:T(8,128)(2,1)}, bf16[256,1024]{1,0:T(8,128)(2,1)}, bf16[1024,1024]{1,0:T(8,128)(2,1)}, bf16[1024,1024]{1,0:T(8,128)(2,1)}) async-done(((bf16[3,1024,256]{2,1,0:T(8,128)(2,1)}, bf16[256,1024]{1,0:T(8,128)(2,1)}, bf16[1024,1024]{1,0:T(8,128)(2,1)}, bf16[1024,1024]{1,0:T(8,128)(2,1)}), (bf16[3,1024,256]{2,1,0:T(8,128)(2,1)}, ...) | async-done | bytes 6291472 | tf_op jit(solution)/shard_map/psum | solution.py:355
  1311.9 127.1 %all-reduce.6.cloned.1.call-done = f32[1024,288]{0,1:T(8,128)} async-done(((f32[1024,288]{0,1:T(8,128)}), f32[1024,288]{0,1:T(8,128)}) %all-reduce.6.cloned.1.call-update) | async-done | bytes 1179664 | tf_op jit(solution)/shard_map/psum | solution.py:357
  (429 shorter events, 223.2 us)
Async XLA Ops:
  10.8 51.1 %all-gather.5.cloned.1.call-start = ((), (), s32[]{:S(2)}) async-start(), calls=%async_computation.6 | async-start | bytes 2621440 | tf_op jit(solution)/shard_map/while/body/eval_jaxpr/all_gather | solution.py:148
  12.7 157.6 %reduce-scatter.5.cloned.1.call-start = ((), (), s32[]{:S(2)}) async-start(), calls=%async_computation.7 | async-start | bytes 5242880 | tf_op jit(solution)/shard_map/while/body/eval_jaxpr/reduce_scatter | solution.py:158
  94.6 75.7 %copy-start.17 = (bf16[2,256,1024]{2,1,0:T(8,128)(2,1)S(1)}, bf16[2,256,1024]{2,1,0:T(8,128)(2,1)}, u32[]{:S(2)}) copy-start(bf16[2,256,1024]{2,1,0:T(8,128)(2,1)} %get-tuple-element.992) | copy-start | bytes 3145732 | tf_op jit(solution)/shard_map/while
  94.6 75.7 %copy-start.50 = (f32[1024]{0:T(1024)S(1)}, f32[1024]{0:T(1024)}, u32[]{:S(2)}) copy-start(f32[1024]{0:T(1024)} %get-tuple-element.996) | copy-start | bytes 12292 | tf_op jit(solution)/shard_map/while
  94.6 77.4 %copy-start.28 = (f32[1024]{0:T(1024)S(1)}, f32[1024]{0:T(1024)}, u32[]{:S(2)}) copy-start(f32[1024]{0:T(1024)} %get-tuple-element.997) | copy-start | bytes 12292 | tf_op jit(solution)/shard_map/while
  94.6 77.4 %copy-start.30 = (f32[1024]{0:T(1024)S(1)}, f32[1024]{0:T(1024)}, u32[]{:S(2)}) copy-start(f32[1024]{0:T(1024)} %get-tuple-element.998) | copy-start | bytes 12292 | tf_op jit(solution)/shard_map/while
  94.6 125.1 %copy-start.58 = (f32[1024]{0:T(1024)S(1)}, f32[1024]{0:T(1024)}, u32[]{:S(2)}) copy-start(f32[1024]{0:T(1024)} %get-tuple-element.1000) | copy-start | bytes 12292 | tf_op jit(solution)/shard_map/while
  94.7 125.1 %all-gather.7.cloned.1.call-start = ((), (), s32[]{:S(2)}) async-start(), calls=%async_computation.8 | async-start | bytes 2621440 | tf_op jit(solution)/shard_map/while/body/eval_jaxpr/all_gather | solution.py:171
  173.1 142.7 %reduce-scatter.7.cloned.1.call-start = ((), (), s32[]{:S(2)}) async-start(), calls=%async_computation.9 | async-start | bytes 5242880 | tf_op jit(solution)/shard_map/while/body/eval_jaxpr/reduce_scatter | solution.py:177
  240.2 75.7 %copy-start.51 = (f32[1024]{0:T(1024)S(1)}, f32[1024]{0:T(1024)}, u32[]{:S(2)}) copy-start(f32[1024]{0:T(1024)} %get-tuple-element.1002) | copy-start | bytes 12292 | tf_op jit(solution)/shard_map/while
  240.2 77.6 %copy-start.31 = (f32[1024]{0:T(1024)S(1)}, f32[1024]{0:T(1024)}, u32[]{:S(2)}) copy-start(f32[1024]{0:T(1024)} %get-tuple-element.1006) | copy-start | bytes 12292 | tf_op jit(solution)/shard_map/while
  240.3 127.8 %all-gather.9.cloned.1.call-start = ((), (), s32[]{:S(2)}) async-start(), calls=%async_computation.10 | async-start | bytes 2621440 | tf_op jit(solution)/shard_map/while/body/eval_jaxpr/all_gather | solution.py:204
  321.4 136.4 %reduce-scatter.9.cloned.1.call-start = ((), (), s32[]{:S(2)}) async-start(), calls=%async_computation.11 | async-start | bytes 5242880 | tf_op jit(solution)/shard_map/while/body/eval_jaxpr/reduce_scatter | solution.py:217
  382.2 125.9 %all-gather.11.cloned.1.call-start = ((), (), s32[]{:S(2)}) async-start(), calls=%async_computation.12 | async-start | bytes 2621440 | tf_op jit(solution)/shard_map/while/body/eval_jaxpr/all_gather | solution.py:234
  461.6 134.5 %reduce-scatter.11.cloned.1.call-start = ((), (), s32[]{:S(2)}) async-start(), calls=%async_computation.13 | async-start | bytes 2621440 | tf_op jit(solution)/shard_map/while/body/eval_jaxpr/reduce_scatter | solution.py:256
  598.5 47.7 %all-gather.5.cloned.1.call-start = ((), (), s32[]{:S(2)}) async-start(), calls=%async_computation.6 | async-start | bytes 2621440 | tf_op jit(solution)/shard_map/while/body/eval_jaxpr/all_gather | solution.py:148
  600.5 154.2 %reduce-scatter.5.cloned.1.call-start = ((), (), s32[]{:S(2)}) async-start(), calls=%async_computation.7 | async-start | bytes 5242880 | tf_op jit(solution)/shard_map/while/body/eval_jaxpr/reduce_scatter | solution.py:158
  679.0 75.7 %copy-start.17 = (bf16[2,256,1024]{2,1,0:T(8,128)(2,1)S(1)}, bf16[2,256,1024]{2,1,0:T(8,128)(2,1)}, u32[]{:S(2)}) copy-start(bf16[2,256,1024]{2,1,0:T(8,128)(2,1)} %get-tuple-element.992) | copy-start | bytes 3145732 | tf_op jit(solution)/shard_map/while
  679.0 75.7 %copy-start.50 = (f32[1024]{0:T(1024)S(1)}, f32[1024]{0:T(1024)}, u32[]{:S(2)}) copy-start(f32[1024]{0:T(1024)} %get-tuple-element.996) | copy-start | bytes 12292 | tf_op jit(solution)/shard_map/while
  679.0 77.4 %copy-start.28 = (f32[1024]{0:T(1024)S(1)}, f32[1024]{0:T(1024)}, u32[]{:S(2)}) copy-start(f32[1024]{0:T(1024)} %get-tuple-element.997) | copy-start | bytes 12292 | tf_op jit(solution)/shard_map/while
  679.0 77.4 %copy-start.30 = (f32[1024]{0:T(1024)S(1)}, f32[1024]{0:T(1024)}, u32[]{:S(2)}) copy-start(f32[1024]{0:T(1024)} %get-tuple-element.998) | copy-start | bytes 12292 | tf_op jit(solution)/shard_map/while
  679.0 125.1 %copy-start.58 = (f32[1024]{0:T(1024)S(1)}, f32[1024]{0:T(1024)}, u32[]{:S(2)}) copy-start(f32[1024]{0:T(1024)} %get-tuple-element.1000) | copy-start | bytes 12292 | tf_op jit(solution)/shard_map/while
  679.0 125.1 %all-gather.7.cloned.1.call-start = ((), (), s32[]{:S(2)}) async-start(), calls=%async_computation.8 | async-start | bytes 2621440 | tf_op jit(solution)/shard_map/while/body/eval_jaxpr/all_gather | solution.py:171
  757.5 142.7 %reduce-scatter.7.cloned.1.call-start = ((), (), s32[]{:S(2)}) async-start(), calls=%async_computation.9 | async-start | bytes 5242880 | tf_op jit(solution)/shard_map/while/body/eval_jaxpr/reduce_scatter | solution.py:177
  824.6 75.7 %copy-start.51 = (f32[1024]{0:T(1024)S(1)}, f32[1024]{0:T(1024)}, u32[]{:S(2)}) copy-start(f32[1024]{0:T(1024)} %get-tuple-element.1002) | copy-start | bytes 12292 | tf_op jit(solution)/shard_map/while
  824.6 77.6 %copy-start.31 = (f32[1024]{0:T(1024)S(1)}, f32[1024]{0:T(1024)}, u32[]{:S(2)}) copy-start(f32[1024]{0:T(1024)} %get-tuple-element.1006) | copy-start | bytes 12292 | tf_op jit(solution)/shard_map/while
  824.6 127.8 %all-gather.9.cloned.1.call-start = ((), (), s32[]{:S(2)}) async-start(), calls=%async_computation.10 | async-start | bytes 2621440 | tf_op jit(solution)/shard_map/while/body/eval_jaxpr/all_gather | solution.py:204
  905.8 136.4 %reduce-scatter.9.cloned.1.call-start = ((), (), s32[]{:S(2)}) async-start(), calls=%async_computation.11 | async-start | bytes 5242880 | tf_op jit(solution)/shard_map/while/body/eval_jaxpr/reduce_scatter | solution.py:217
  966.6 125.9 %all-gather.11.cloned.1.call-start = ((), (), s32[]{:S(2)}) async-start(), calls=%async_computation.12 | async-start | bytes 2621440 | tf_op jit(solution)/shard_map/while/body/eval_jaxpr/all_gather | solution.py:234
  1045.9 134.6 %reduce-scatter.11.cloned.1.call-start = ((), (), s32[]{:S(2)}) async-start(), calls=%async_computation.13 | async-start | bytes 2621440 | tf_op jit(solution)/shard_map/while/body/eval_jaxpr/reduce_scatter | solution.py:256
  1185.7 115.6 %all-reduce.8.cloned.1.call-start = ((), (), s32[]{:S(2)}) async-start(), calls=%async_computation.5 | async-start | bytes 12582912 | tf_op jit(solution)/shard_map/psum | solution.py:355
  1196.6 242.5 %all-reduce.6.cloned.1.call-start = ((), (), s32[]{:S(2)}) async-start(), calls=%async_computation.4 | async-start | bytes 2359296 | tf_op jit(solution)/shard_map/psum | solution.py:357
  (101 other events, 699.8 us)
Sparse Core Ops, SparseCore 0:
  13.2 48.6 all-gather.4
  94.8 75.4 reduce-scatter.4
  173.3 46.4 all-gather.6
  240.4 75.4 reduce-scatter.6
  321.6 46.4 all-gather.8
  382.4 75.4 reduce-scatter.8
  461.7 46.4 all-gather.10
  553.5 42.5 reduce-scatter.10
  600.9 45.2 all-gather.4
  679.1 75.4 reduce-scatter.4
  757.6 46.4 all-gather.6
  824.7 75.4 reduce-scatter.6
  905.9 46.4 all-gather.8
  966.7 75.4 reduce-scatter.8
  1046.0 46.4 all-gather.10
  1137.9 42.5 reduce-scatter.10
Sparse Core Ops, SparseCore 1:
  1196.7 104.6 all-reduce.7
  1308.1 130.9 all-reduce.5
where the time goes:
time: 1450 us
  waiting for transfers between devices  1030 us (71%)
  matrix products  209 us (14%)
  other arithmetic  99.4 us (7%)
  blocking collectives  54.2 us (4%)
  local copies, waits for them, and re-layouts  33.1 us (2%)
  between operations  15.6 us (1%)
    reduce_scatter x2, waiting for transfers between devices, process(): lax.psum_scatter(jnp.einsum('nf,df->nd', device_rows(grad_hidden, lax.axi...  151 us
    reduce_scatter x2, waiting for transfers between devices, process(): lax.psum_scatter(jnp.dot(device_rows(active, lax.axis_size('tensor') * (g...  151 us
    reduce_scatter x2, waiting for transfers between devices, process(): lax.psum_scatter(jnp.dot(device_rows(mixed, lax.axis_size('tensor') * (gr...  150 us
    psum x1, waiting for transfers between devices, per_device(): shared_grads = lax.psum(shared_grads, ('dp', 'tensor'))  127 us
    all_gather x2, waiting for transfers between devices, process(): lax.all_gather(normed.astype(jnp.bfloat16), 'tensor', axis=1, tiled=True)  93.1 us
    all_gather x2, waiting for transfers between devices, process(): whole_first = lax.all_gather(first_low, 'tensor', axis=1, tiled=True)  93 us
    all_gather x2, waiting for transfers between devices, process(): whole_second = lax.all_gather(second_low, 'tensor', axis=1, tiled=True)  92.3 us
    all_gather x2, waiting for transfers between devices, process(): whole_tokens = lax.all_gather(tokens, 'tensor', axis=1, tiled=True)  85.2 us
  transfers between devices with their start and end apart: 18, of which 18 were waited for; matrix products, arithmetic and copies ran while one was open for 4% of the time, Pallas kernels for 0%

commit v1 on v0

--- a/solution.py
+++ b/solution.py
@@ -231,7 +231,19 @@
     )
     first_low = grad_first.astype(jnp.bfloat16)
     out_bias_grad = jnp.sum(first_low.astype(jnp.float32), axis=(0, 1))
-    whole_first = lax.all_gather(first_low, "tensor", axis=1, tiled=True)
+    p_count = lax.axis_size("tensor")
+    kept_rows = [(h, (h + 1) % p_count) for h in range(p_count)]
+    block_list = [(h, (h - 1) % p_count) for h in range(p_count)]
+    before, u1 = ([first_low], [first_low])
+    for _ in range(p_count // 2):
+        low = lax.ppermute(before[-1], axis_name="tensor", perm=kept_rows)
+        before.append(low)
+    for _ in tuple(range((p_count - 1) // 2)):
+        opened = lax.ppermute(u1[-1], axis_name="tensor", perm=block_list)
+        u1.append(opened)
+    near = jnp.concatenate([*before[::-1], *u1[1:]], 1)
+    local_part = lax.axis_index("tensor")
+    whole_first = jnp.roll(near, (local_part - p_count // 2) * first_low.shape[1], 1)
     out_weight_grad = jnp.einsum(
         "glh,gld->hd", mixed, whole_first, preferred_element_type=jnp.float32
     )

time: 1450 us -> 1450 us (level)
  waiting for transfers between devices: 1030 us -> 1010 us
    all_gather x2 -> x0, waiting for transfers between devices: 93 us -> none  [process(): whole_first = lax.all_gather(first_low, 'tensor', axis=1, tiled=True)]
    ppermute x0 -> x6, waiting for transfers between devices: none -> 64.5 us  [the longest x4 53.8 us: process(): low = lax.ppermute(before[-1], axis_name='tensor', perm=kept_rows)]
    while x212 -> x254, local copies, waits for them, and re-layouts: 18.8 us -> 30.1 us
  transfers between devices with their start and end apart: 18 -> 22, of which waited for: 18 -> 22; matrix products, arithmetic and copies ran while one was open for 4% -> 4% of each run, Pallas kernels for 0% -> 0%
where the time goes in v1:
time: 1450 us; the launch traced here: 1440 us
  waiting for transfers between devices  1010 us (70%)
  matrix products  205 us (14%)
  other arithmetic  99.1 us (7%)
  blocking collectives  54.2 us (4%)
  local copies, waits for them, and re-layouts  44.5 us (3%)
  between operations  15.6 us (1%)
    reduce_scatter x2, waiting for transfers between devices, process(): lax.psum_scatter(jnp.einsum('nf,df->nd', device_rows(grad_hidden, lax.axi...  151 us
    reduce_scatter x2, waiting for transfers between devices, process(): lax.psum_scatter(jnp.dot(device_rows(active, lax.axis_size('tensor') * (g...  151 us
    reduce_scatter x2, waiting for transfers between devices, process(): lax.psum_scatter(jnp.dot(device_rows(mixed, lax.axis_size('tensor') * (gr...  150 us
    psum x1, waiting for transfers between devices, per_device(): shared_grads = lax.psum(shared_grads, ('dp', 'tensor'))  127 us
    all_gather x2, waiting for transfers between devices, process(): lax.all_gather(normed.astype(jnp.bfloat16), 'tensor', axis=1, tiled=True)  93.1 us
    all_gather x2, waiting for transfers between devices, process(): whole_second = lax.all_gather(second_low, 'tensor', axis=1, tiled=True)  92.5 us
    all_gather x2, waiting for transfers between devices, process(): whole_tokens = lax.all_gather(tokens, 'tensor', axis=1, tiled=True)  85.1 us
    ppermute x4, waiting for transfers between devices, process(): low = lax.ppermute(before[-1], axis_name='tensor', perm=kept_rows)  53.8 us
  transfers between devices with their start and end apart: 22, of which 22 were waited for; matrix products, arithmetic and copies ran while one was open for 4% of the time, Pallas kernels for 0%

profile of v1, /device:TPU:0, one launch (start us, length us, event | category | flops | bytes accessed | tf_op | source)
XLA Modules:
  0.0 1442.6 jit_solution(17659754128190948934)
XLA Ops:
  10.8 1168.6 %while.8 = (s32[]{:T(128)}, f32[3,1024,256]{1,2,0:T(8,128)}, f32[3,256]{1,0:T(4,128)}, f32[256,1024]{1,0:T(8,128)}, f32[1024,1024]{1,0:T(8,128)}, /*index=5*/f32...) while((s32[]{:T(128)}, f32[3,1024,256]{1,2,0:T(8,128)}, ...), condition=%wide.region_26.27_spmd.clone, body=%wide.region_0.26_spmd.clone.sunk | while | flops 23216961536 | bytes 667883968 | solution.py:363
  17.6 44.3 %all-gather.4.cloned.1.call-done = bf16[1,1024,1024]{2,1,0:T(8,128)(2,1)} async-done(((bf16[1,256,1024]{2,1,0:T(8,128)(2,1)}), bf16[1,1024,1024]{2,1,0:T(8,128)(2,1)}) %all-gather.4.cloned.1.call-update) | async-done | bytes 2097168 | tf_op jit(solution)/shard_map/while/body/eval_jaxpr/all_gather | solution.py:148
  74.1 8.8 fusion.231
  95.2 75.1 %reduce-scatter.5.cloned.1.call-done = f32[256,1024]{1,0:T(8,128)} async-done(((f32[1024,1024]{1,0:T(8,128)}), f32[256,1024]{1,0:T(8,128)}) %reduce-scatter.5.cloned.1.call-update) | async-done | bytes 1048592 | tf_op jit(solution)/shard_map/while/body/eval_jaxpr/reduce_scatter | solution.py:158
  173.2 46.5 %all-gather.6.cloned.1.call-done = bf16[1,1024,1024]{2,1,0:T(8,128)(2,1)} async-done(((bf16[1,256,1024]{2,1,0:T(8,128)(2,1)}), bf16[1,1024,1024]{2,1,0:T(8,128)(2,1)}) %all-gather.6.cloned.1.call-update) | async-done | bytes 2097168 | tf_op jit(solution)/shard_map/while/body/eval_jaxpr/all_gather | solution.py:171
  219.7 14.9 %multiply_convert_fusion.4 = (bf16[1024,1024]{1,0:T(8,128)(2,1)S(1)}, f32[1024,1024]{1,0:T(8,128)}, f32[1024,1024]{1,0:T(8,128)}) fusion(f32[1024]{0:T(1024)S(1)} %copy-done.65, bf16[1024,1024]{1,0:T(8,128)(2,1)} %get-tuple-element.1255, bf16[1,1024,1024]{2,1,0:T(8,128)(2,1)} %all-gather.6.cloned.1.call-done), kind=kOutput, calls=%fused_computation.17.clone.1 | convolution fusion | flops 2216689664 | bytes 14684160 | tf_op jit(solution)/shard_map/while/body/eval_jaxpr/gld,df->glf/dot_general | solution.py:173
  240.4 75.6 %reduce-scatter.7.cloned.1.call-done = f32[256,1024]{1,0:T(8,128)} async-done(((f32[1024,1024]{1,0:T(8,128)}), f32[256,1024]{1,0:T(8,128)}) %reduce-scatter.7.cloned.1.call-update) | async-done | bytes 1048592 | tf_op jit(solution)/shard_map/while/body/eval_jaxpr/reduce_scatter | solution.py:177
  321.8 46.4 %all-gather.8.cloned.1.call-done = bf16[1,1024,1024]{2,1,0:T(8,128)(2,1)} async-done(((bf16[1,256,1024]{2,1,0:T(8,128)(2,1)}), bf16[1,1024,1024]{2,1,0:T(8,128)(2,1)}) %all-gather.8.cloned.1.call-update) | async-done | bytes 2097168 | tf_op jit(solution)/shard_map/while/body/eval_jaxpr/all_gather | solution.py:204
  382.4 75.6 %reduce-scatter.9.cloned.1.call-done = f32[256,1024]{1,0:T(8,128)} async-done(((f32[1024,1024]{1,0:T(8,128)}), f32[256,1024]{1,0:T(8,128)}) %reduce-scatter.9.cloned.1.call-update) | async-done | bytes 1048592 | tf_op jit(solution)/shard_map/while/body/eval_jaxpr/reduce_scatter | solution.py:217
  463.7 14.0 collective-permute-done
  481.6 12.9 collective-permute-done.1
  514.1 11.8 multiply_reduce_fusion.18
  526.0 12.3 multiply_convert_fusion.5
  570.8 22.2 %reduce-scatter.11.cloned.1.call-done = bf16[256,1024]{1,0:T(8,128)(2,1)} async-done(((bf16[1024,1024]{1,0:T(8,128)(2,1)}), bf16[256,1024]{1,0:T(8,128)(2,1)}) %reduce-scatter.11.cloned.1.call-update) | async-done | bytes 524304 | tf_op jit(solution)/shard_map/while/body/eval_jaxpr/reduce_scatter | solution.py:268
  602.1 40.9 %all-gather.4.cloned.1.call-done = bf16[1,1024,1024]{2,1,0:T(8,128)(2,1)} async-done(((bf16[1,256,1024]{2,1,0:T(8,128)(2,1)}), bf16[1,1024,1024]{2,1,0:T(8,128)(2,1)}) %all-gather.4.cloned.1.call-update) | async-done | bytes 2097168 | tf_op jit(solution)/shard_map/while/body/eval_jaxpr/all_gather | solution.py:148
  655.2 8.8 fusion.231
  676.0 75.4 %reduce-scatter.5.cloned.1.call-done = f32[256,1024]{1,0:T(8,128)} async-done(((f32[1024,1024]{1,0:T(8,128)}), f32[256,1024]{1,0:T(8,128)}) %reduce-scatter.5.cloned.1.call-update) | async-done | bytes 1048592 | tf_op jit(solution)/shard_map/while/body/eval_jaxpr/reduce_scatter | solution.py:158
  754.3 46.6 %all-gather.6.cloned.1.call-done = bf16[1,1024,1024]{2,1,0:T(8,128)(2,1)} async-done(((bf16[1,256,1024]{2,1,0:T(8,128)(2,1)}), bf16[1,1024,1024]{2,1,0:T(8,128)(2,1)}) %all-gather.6.cloned.1.call-update) | async-done | bytes 2097168 | tf_op jit(solution)/shard_map/while/body/eval_jaxpr/all_gather | solution.py:171
  800.8 14.9 %multiply_convert_fusion.4 = (bf16[1024,1024]{1,0:T(8,128)(2,1)S(1)}, f32[1024,1024]{1,0:T(8,128)}, f32[1024,1024]{1,0:T(8,128)}) fusion(f32[1024]{0:T(1024)S(1)} %copy-done.65, bf16[1024,1024]{1,0:T(8,128)(2,1)} %get-tuple-element.1255, bf16[1,1024,1024]{2,1,0:T(8,128)(2,1)} %all-gather.6.cloned.1.call-done), kind=kOutput, calls=%fused_computation.17.clone.1 | convolution fusion | flops 2216689664 | bytes 14684160 | tf_op jit(solution)/shard_map/while/body/eval_jaxpr/gld,df->glf/dot_general | solution.py:173
  821.5 75.6 %reduce-scatter.7.cloned.1.call-done = f32[256,1024]{1,0:T(8,128)} async-done(((f32[1024,1024]{1,0:T(8,128)}), f32[256,1024]{1,0:T(8,128)}) %reduce-scatter.7.cloned.1.call-update) | async-done | bytes 1048592 | tf_op jit(solution)/shard_map/while/body/eval_jaxpr/reduce_scatter | solution.py:177
  903.1 46.2 %all-gather.8.cloned.1.call-done = bf16[1,1024,1024]{2,1,0:T(8,128)(2,1)} async-done(((bf16[1,256,1024]{2,1,0:T(8,128)(2,1)}), bf16[1,1024,1024]{2,1,0:T(8,128)(2,1)}) %all-gather.8.cloned.1.call-update) | async-done | bytes 2097168 | tf_op jit(solution)/shard_map/while/body/eval_jaxpr/all_gather | solution.py:204
  963.5 75.6 %reduce-scatter.9.cloned.1.call-done = f32[256,1024]{1,0:T(8,128)} async-done(((f32[1024,1024]{1,0:T(8,128)}), f32[256,1024]{1,0:T(8,128)}) %reduce-scatter.9.cloned.1.call-update) | async-done | bytes 1048592 | tf_op jit(solution)/shard_map/while/body/eval_jaxpr/reduce_scatter | solution.py:217
  1044.8 14.0 collective-permute-done
  1062.7 12.9 collective-permute-done.1
  1086.5 8.7 fusion.240
  1095.3 11.8 multiply_reduce_fusion.18
  1107.1 12.2 multiply_convert_fusion.5
  1155.0 19.0 %reduce-scatter.11.cloned.1.call-done = bf16[256,1024]{1,0:T(8,128)(2,1)} async-done(((bf16[1024,1024]{1,0:T(8,128)(2,1)}), bf16[256,1024]{1,0:T(8,128)(2,1)}) %reduce-scatter.11.cloned.1.call-update) | async-done | bytes 524304 | tf_op jit(solution)/shard_map/while/body/eval_jaxpr/reduce_scatter | solution.py:268
  1190.9 13.8 all-reduce.1
  1205.9 40.5 %all-reduce = (f32[1024]{0:T(1024)}, f32[1024]{0:T(1024)}, f32[1024]{0:T(1024)}, f32[1024]{0:T(1024)}, f32[1024]{0:T(1024)}, /*index=5*/f32[1024]{0:T(1024)}) all-reduce(f32[1024]{0:T(1024)S(1)} %copy-done.54, f32[1024]{0:T(1024)S(1)} %copy-done.51, f32[1024]{0:T(1024)S(1)} %copy-done.48, ...), channel_id=1, replica_groups=mesh['dp'=8,'tensor'=4] {'dp','tensor'}, use_global_device_ids=true, to_apply=%region_30.31 | all-reduce | flops 6144 | bytes 49152 | tf_op jit(solution)/shard_map/psum | solution.py:369
  1246.4 48.6 %all-reduce.8.cloned.1.call-done = (bf16[3,1024,256]{2,1,0:T(8,128)(2,1)}, bf16[256,1024]{1,0:T(8,128)(2,1)}, bf16[1024,1024]{1,0:T(8,128)(2,1)}, bf16[1024,1024]{1,0:T(8,128)(2,1)}) async-done(((bf16[3,1024,256]{2,1,0:T(8,128)(2,1)}, bf16[256,1024]{1,0:T(8,128)(2,1)}, bf16[1024,1024]{1,0:T(8,128)(2,1)}, bf16[1024,1024]{1,0:T(8,128)(2,1)}), (bf16[3,1024,256]{2,1,0:T(8,128)(2,1)}, ...) | async-done | bytes 6291472 | tf_op jit(solution)/shard_map/psum | solution.py:367
  1305.6 127.1 %all-reduce.6.cloned.1.call-done = f32[1024,288]{0,1:T(8,128)} async-done(((f32[1024,288]{0,1:T(8,128)}), f32[1024,288]{0,1:T(8,128)}) %all-reduce.6.cloned.1.call-update) | async-done | bytes 1179664 | tf_op jit(solution)/shard_map/psum | solution.py:369
  (479 shorter events, 269.0 us)
Async XLA Ops:
  10.8 51.1 %all-gather.4.cloned.1.call-start = ((), (), s32[]{:S(2)}) async-start(), calls=%async_computation.6 | async-start | bytes 2621440 | tf_op jit(solution)/shard_map/while/body/eval_jaxpr/all_gather | solution.py:148
  12.7 157.6 %reduce-scatter.5.cloned.1.call-start = ((), (), s32[]{:S(2)}) async-start(), calls=%async_computation.7 | async-start | bytes 5242880 | tf_op jit(solution)/shard_map/while/body/eval_jaxpr/reduce_scatter | solution.py:158
  94.6 75.7 %copy-start.20 = (bf16[2,256,1024]{2,1,0:T(8,128)(2,1)S(1)}, bf16[2,256,1024]{2,1,0:T(8,128)(2,1)}, u32[]{:S(2)}) copy-start(bf16[2,256,1024]{2,1,0:T(8,128)(2,1)} %get-tuple-element.1248) | copy-start | bytes 3145732 | tf_op jit(solution)/shard_map/while
  94.6 75.7 %copy-start.55 = (f32[1024]{0:T(1024)S(1)}, f32[1024]{0:T(1024)}, u32[]{:S(2)}) copy-start(f32[1024]{0:T(1024)} %get-tuple-element.1252) | copy-start | bytes 12292 | tf_op jit(solution)/shard_map/while
  94.6 77.4 %copy-start.34 = (f32[1024]{0:T(1024)S(1)}, f32[1024]{0:T(1024)}, u32[]{:S(2)}) copy-start(f32[1024]{0:T(1024)} %get-tuple-element.1253) | copy-start | bytes 12292 | tf_op jit(solution)/shard_map/while
  94.6 77.4 %copy-start.35 = (f32[1024]{0:T(1024)S(1)}, f32[1024]{0:T(1024)}, u32[]{:S(2)}) copy-start(f32[1024]{0:T(1024)} %get-tuple-element.1254) | copy-start | bytes 12292 | tf_op jit(solution)/shard_map/while
  94.6 125.1 %copy-start.65 = (f32[1024]{0:T(1024)S(1)}, f32[1024]{0:T(1024)}, u32[]{:S(2)}) copy-start(f32[1024]{0:T(1024)} %get-tuple-element.1256) | copy-start | bytes 12292 | tf_op jit(solution)/shard_map/while
  94.6 125.1 %all-gather.6.cloned.1.call-start = ((), (), s32[]{:S(2)}) async-start(), calls=%async_computation.8 | async-start | bytes 2621440 | tf_op jit(solution)/shard_map/while/body/eval_jaxpr/all_gather | solution.py:171
  173.1 142.8 %reduce-scatter.7.cloned.1.call-start = ((), (), s32[]{:S(2)}) async-start(), calls=%async_computation.9 | async-start | bytes 5242880 | tf_op jit(solution)/shard_map/while/body/eval_jaxpr/reduce_scatter | solution.py:177
  240.3 77.6 %copy-start.36 = (f32[1024]{0:T(1024)S(1)}, f32[1024]{0:T(1024)}, u32[]{:S(2)}) copy-start(f32[1024]{0:T(1024)} %get-tuple-element.1262) | copy-start | bytes 12292 | tf_op jit(solution)/shard_map/while
  240.3 127.8 %all-gather.8.cloned.1.call-start = ((), (), s32[]{:S(2)}) async-start(), calls=%async_computation.10 | async-start | bytes 2621440 | tf_op jit(solution)/shard_map/while/body/eval_jaxpr/all_gather | solution.py:204
  321.5 136.5 %reduce-scatter.9.cloned.1.call-start = ((), (), s32[]{:S(2)}) async-start(), calls=%async_computation.11 | async-start | bytes 5242880 | tf_op jit(solution)/shard_map/while/body/eval_jaxpr/reduce_scatter | solution.py:217
  382.3 210.6 %reduce-scatter.11.cloned.1.call-start = ((), (), s32[]{:S(2)}) async-start(), calls=%async_computation.12 | async-start | bytes 2621440 | tf_op jit(solution)/shard_map/while/body/eval_jaxpr/reduce_scatter | solution.py:268
  462.2 15.5 %collective-permute-start = (bf16[1,256,1024]{2,1,0:T(8,128)(2,1)S(1)}, bf16[1,256,1024]{2,1,0:T(8,128)(2,1)S(1)}, u32[]{:S(2)}, u32[]{:S(2)}) collective-permute-start(bf16[1,256,1024]{2,1,0:T(8,128)(2,1)S(1)} %get-tuple-element.1114), channel_id=1, source_target_pairs={{0,1},{1,2},{2,3},{3,0},{4,5},{5,6},{6,7},{7,4},{8,9},{9,10},{10,1... | collective-permute-start | bytes 1572872 | tf_op jit(solution)/shard_map/while/body/eval_jaxpr/ppermute | solution.py:239
  477.7 16.8 %collective-permute-start.1 = (bf16[1,256,1024]{2,1,0:T(8,128)(2,1)S(1)}, bf16[1,256,1024]{2,1,0:T(8,128)(2,1)}, u32[]{:S(2)}, u32[]{:S(2)}) collective-permute-start(bf16[1,256,1024]{2,1,0:T(8,128)(2,1)S(1)} %collective-permute-done), channel_id=1, source_target_pairs={{0,1},{1,2},{2,3},{3,0},{4,5},{5,6},{6,7},{7,4},{8,9},{9,10},{10,1... | collective-permute-start | bytes 1572872 | tf_op jit(solution)/shard_map/while/body/eval_jaxpr/ppermute | solution.py:239
  477.7 24.3 %collective-permute-start.2 = (bf16[1,256,1024]{2,1,0:T(8,128)(2,1)}, bf16[1,256,1024]{2,1,0:T(8,128)(2,1)S(1)}, u32[]{:S(2)}, u32[]{:S(2)}) collective-permute-start(bf16[1,256,1024]{2,1,0:T(8,128)(2,1)} %copy-done.4), channel_id=1, source_target_pairs={{0,3},{1,0},{2,1},{3,2},{4,7},{5,4},{6,5},{7,6},{8,11},{9,8},{10,9... | collective-permute-start | bytes 1572872 | tf_op jit(solution)/shard_map/while/body/eval_jaxpr/ppermute | solution.py:242
  595.2 47.7 %all-gather.4.cloned.1.call-start = ((), (), s32[]{:S(2)}) async-start(), calls=%async_computation.6 | async-start | bytes 2621440 | tf_op jit(solution)/shard_map/while/body/eval_jaxpr/all_gather | solution.py:148
  597.2 154.2 %reduce-scatter.5.cloned.1.call-start = ((), (), s32[]{:S(2)}) async-start(), calls=%async_computation.7 | async-start | bytes 5242880 | tf_op jit(solution)/shard_map/while/body/eval_jaxpr/reduce_scatter | solution.py:158
  675.7 77.4 %copy-start.34 = (f32[1024]{0:T(1024)S(1)}, f32[1024]{0:T(1024)}, u32[]{:S(2)}) copy-start(f32[1024]{0:T(1024)} %get-tuple-element.1253) | copy-start | bytes 12292 | tf_op jit(solution)/shard_map/while
  675.7 77.4 %copy-start.35 = (f32[1024]{0:T(1024)S(1)}, f32[1024]{0:T(1024)}, u32[]{:S(2)}) copy-start(f32[1024]{0:T(1024)} %get-tuple-element.1254) | copy-start | bytes 12292 | tf_op jit(solution)/shard_map/while
  675.7 125.1 %copy-start.65 = (f32[1024]{0:T(1024)S(1)}, f32[1024]{0:T(1024)}, u32[]{:S(2)}) copy-start(f32[1024]{0:T(1024)} %get-tuple-element.1256) | copy-start | bytes 12292 | tf_op jit(solution)/shard_map/while
  675.8 125.1 %all-gather.6.cloned.1.call-start = ((), (), s32[]{:S(2)}) async-start(), calls=%async_computation.8 | async-start | bytes 2621440 | tf_op jit(solution)/shard_map/while/body/eval_jaxpr/all_gather | solution.py:171
  754.2 142.8 %reduce-scatter.7.cloned.1.call-start = ((), (), s32[]{:S(2)}) async-start(), calls=%async_computation.9 | async-start | bytes 5242880 | tf_op jit(solution)/shard_map/while/body/eval_jaxpr/reduce_scatter | solution.py:177
  821.4 77.6 %copy-start.36 = (f32[1024]{0:T(1024)S(1)}, f32[1024]{0:T(1024)}, u32[]{:S(2)}) copy-start(f32[1024]{0:T(1024)} %get-tuple-element.1262) | copy-start | bytes 12292 | tf_op jit(solution)/shard_map/while
  821.4 127.8 %all-gather.8.cloned.1.call-start = ((), (), s32[]{:S(2)}) async-start(), calls=%async_computation.10 | async-start | bytes 2621440 | tf_op jit(solution)/shard_map/while/body/eval_jaxpr/all_gather | solution.py:204
  902.7 136.4 %reduce-scatter.9.cloned.1.call-start = ((), (), s32[]{:S(2)}) async-start(), calls=%async_computation.11 | async-start | bytes 5242880 | tf_op jit(solution)/shard_map/while/body/eval_jaxpr/reduce_scatter | solution.py:217
  963.5 210.6 %reduce-scatter.11.cloned.1.call-start = ((), (), s32[]{:S(2)}) async-start(), calls=%async_computation.12 | async-start | bytes 2621440 | tf_op jit(solution)/shard_map/while/body/eval_jaxpr/reduce_scatter | solution.py:268
  1043.3 15.5 %collective-permute-start = (bf16[1,256,1024]{2,1,0:T(8,128)(2,1)S(1)}, bf16[1,256,1024]{2,1,0:T(8,128)(2,1)S(1)}, u32[]{:S(2)}, u32[]{:S(2)}) collective-permute-start(bf16[1,256,1024]{2,1,0:T(8,128)(2,1)S(1)} %get-tuple-element.1114), channel_id=1, source_target_pairs={{0,1},{1,2},{2,3},{3,0},{4,5},{5,6},{6,7},{7,4},{8,9},{9,10},{10,1... | collective-permute-start | bytes 1572872 | tf_op jit(solution)/shard_map/while/body/eval_jaxpr/ppermute | solution.py:239
  1058.8 16.8 %collective-permute-start.1 = (bf16[1,256,1024]{2,1,0:T(8,128)(2,1)S(1)}, bf16[1,256,1024]{2,1,0:T(8,128)(2,1)}, u32[]{:S(2)}, u32[]{:S(2)}) collective-permute-start(bf16[1,256,1024]{2,1,0:T(8,128)(2,1)S(1)} %collective-permute-done), channel_id=1, source_target_pairs={{0,1},{1,2},{2,3},{3,0},{4,5},{5,6},{6,7},{7,4},{8,9},{9,10},{10,1... | collective-permute-start | bytes 1572872 | tf_op jit(solution)/shard_map/while/body/eval_jaxpr/ppermute | solution.py:239
  1058.9 24.3 %collective-permute-start.2 = (bf16[1,256,1024]{2,1,0:T(8,128)(2,1)}, bf16[1,256,1024]{2,1,0:T(8,128)(2,1)S(1)}, u32[]{:S(2)}, u32[]{:S(2)}) collective-permute-start(bf16[1,256,1024]{2,1,0:T(8,128)(2,1)} %copy-done.4), channel_id=1, source_target_pairs={{0,3},{1,0},{2,1},{3,2},{4,7},{5,4},{6,5},{7,6},{8,11},{9,8},{10,9... | collective-permute-start | bytes 1572872 | tf_op jit(solution)/shard_map/while/body/eval_jaxpr/ppermute | solution.py:242
  1179.3 115.7 %all-reduce.8.cloned.1.call-start = ((), (), s32[]{:S(2)}) async-start(), calls=%async_computation.5 | async-start | bytes 12582912 | tf_op jit(solution)/shard_map/psum | solution.py:367
  1190.3 242.5 %all-reduce.6.cloned.1.call-start = ((), (), s32[]{:S(2)}) async-start(), calls=%async_computation.4 | async-start | bytes 2359296 | tf_op jit(solution)/shard_map/psum | solution.py:369
  (119 other events, 1139.5 us)
Sparse Core Ops, SparseCore 0:
  13.2 48.6 all-gather.3
  94.8 75.4 reduce-scatter.4
  173.2 46.4 all-gather.5
  240.4 75.4 reduce-scatter.6
  321.6 46.4 all-gather.7
  382.5 75.4 reduce-scatter.8
  549.3 43.5 reduce-scatter.10
  597.7 45.2 all-gather.3
  675.9 75.4 reduce-scatter.4
  754.3 46.4 all-gather.5
  821.6 75.4 reduce-scatter.6
  902.8 46.4 all-gather.7
  963.6 75.4 reduce-scatter.8
  1130.4 43.5 reduce-scatter.10
Sparse Core Ops, SparseCore 1:
  1190.4 104.6 all-reduce.7
  1301.7 130.9 all-reduce.5
